TPU v7x, 32 devices: a whole 2x2x4 slice. The times are simulated.
32 devices in a mesh: mem: 2 (over x), col: 16 (over z, y, core).
Axes of the slice: x: 2, y: 2, z: 4, core: 2. Of those that a mesh axis runs over, the one named last changes fastest.
Arguments:
- perturbations: bfloat16 [2, 16, 384, 768], P('mem', None, 'col'), may hold values from -6 to 6
- gradient: float32 [16, 384, 768], P(None, 'col'), may hold values from -6 to 6
- member_weights: float32 [2], P('mem'), may hold values from 0.5 to 2
- scale_weights: float32 [3], replicated, may hold values from 0.2 to 2
- lon_filter: bfloat16 [3, 768, 768], P(None, 'mem'), may hold values from -1 to 1.5
- lat_filter: bfloat16 [3, 384, 384], P(None, 'col'), may hold values from -1 to 1.5
Outputs:
- increment: float32 [16, 384, 768], P('mem', 'col')
All inputs are finite; a program needn't handle non-finite values.
Results may differ from a plain program's by a relative error of at most 0.01.
Values may be sent and summed in bfloat16 or wider, within the bound.
A program may use at most 64 MiB of HBM per device.

v0:
```python
import jax
import jax.numpy as jnp
from jax import lax
from jax.sharding import PartitionSpec as P


def on_device(perturbations, gradient, member_weights, scale_weights, lon_filter, lat_filter):
    member = perturbations[0].astype(jnp.float32)
    schur = (member * gradient).astype(jnp.bfloat16)
    levels = lax.all_to_all(schur, "col", split_axis=0, concat_axis=1, tiled=True)
    along = jnp.einsum(
        "laj,sij->lsai",
        levels,
        lax.all_gather(lon_filter, "mem", axis=1, tiled=True),
        preferred_element_type=jnp.float32,
    ).astype(jnp.bfloat16)
    across = jnp.einsum(
        "sab,lsbi->lsai",
        lax.all_gather(lat_filter, "col", axis=1, tiled=True),
        along,
        preferred_element_type=jnp.float32,
    )
    filtered = jnp.einsum("s,lsai->lai", scale_weights, across).astype(jnp.bfloat16)
    back = lax.all_to_all(filtered, "col", split_axis=1, concat_axis=0, tiled=True)
    terms = member_weights[0] * member * back.astype(jnp.float32)
    return lax.psum_scatter(terms, "mem", scatter_dimension=0, tiled=True)


def solution(mesh):
    placed = (
        P("mem", None, "col", None),
        P(None, "col", None),
        P("mem"),
        P(),
        P(None, "mem", None),
        P(None, "col", None),
    )
    return jax.shard_map(
        on_device, mesh=mesh, in_specs=placed, out_specs=P("mem", "col", None), check_vma=False
    )
```

profile of v0, /device:TPU:0, one launch (start us, length us, event | category | flops | bytes accessed | tf_op | source)
XLA Modules:
  0.0 129.6 jit_solution(12170853550535788724)
XLA Ops:
  6.5 0.0 copy-start
  6.5 0.0 copy-start.1
  6.5 0.0 copy-start.2
  6.5 0.0 all-gather.2.cloned.1.call-start
  6.5 0.7 all-gather.2.cloned.1.call-update
  7.3 0.4 copy-done.1
  7.6 0.4 copy-done.2
  8.0 0.0 copy-start.3
  8.0 0.9 fusion.5
  8.9 7.4 %all-to-all-start = ((bf16[16,24,768]{2,1,0:T(8,128)(2,1)}), bf16[16,24,768]{2,1,0:T(8,128)(2,1)S(1)}, u32[]{:S(2)}, u32[]{:S(2)}) async-start(bf16[16,24,768]{2,1,0:T(8,128)(2,1)} %fusion.5), calls=%async_computation | async-start | bytes 1179648 | tf_op jit(solution)/shard_map/all_to_all | solution.py:10
  16.4 0.0 copy-done.3
  16.4 29.1 %all_gather.7 = bf16[3,384,384]{2,1,0:T(8,128)(2,1)S(1)} all-gather(bf16[3,24,384]{2,1,0:T(8,128)(2,1)S(1)} %copy-done.3), channel_id=1, replica_groups=mesh['mem'=2,'col'=16] {'col'}, dimensions={1}, use_global_device_ids=true | all-gather | bytes 940032 | tf_op jit(solution)/shard_map/all_gather | solution.py:19
  45.5 0.0 all-to-all-done
  45.5 15.5 %all-gather.2.cloned.1.call-done = bf16[3,768,768]{2,1,0:T(8,128)(2,1)} async-done(((bf16[3,384,768]{2,1,0:T(8,128)(2,1)}), bf16[3,768,768]{2,1,0:T(8,128)(2,1)}) %all-gather.2.cloned.1.call-update) | async-done | bytes 3538960 | tf_op jit(solution)/shard_map/all_gather | solution.py:14
  61.0 5.9 %convolution_bitcast_fusion = bf16[3,384,768]{1,2,0:T(8,128)(2,1)} fusion(bf16[3,384,384]{2,1,0:T(8,128)(2,1)S(1)} %all_gather.7, bf16[384,768,1]{1,0,2:T(8,128)(2,1)S(1)} %bitcast.56, bf16[3,768,768]{2,1,0:T(8,128)(2,1)} %all-gather.2.cloned.1.call-done), kind=kOutput, calls=%fused_computation | convolution fusion | flops 2039316480 | bytes 6782976 | tf_op jit(solution)/shard_map/sab,lsbi->lsai/dot_general | solution.py:17
  66.9 4.0 %copy.12 = bf16[3,384,768]{2,0,1:T(4,128)(2,1)S(1)} copy(bf16[3,384,768]{1,2,0:T(8,128)(2,1)} %convolution_bitcast_fusion) | data formatting | bytes 3538944 | tf_op jit(solution)/shard_map/reshape.6
  70.9 0.0 copy-done
  70.9 1.4 %fusion.10 = bf16[1,384,768]{2,0,1:T(2,128)(2,1)S(1)} fusion(bf16[3,384,768]{2,0,1:T(4,128)(2,1)S(1)} %copy.12, f32[3]{0:T(128)S(1)} %copy-done), kind=kOutput, calls=%fused_computation.13 | convolution fusion | flops 1769472 | bytes 2359308 | tf_op jit(solution)/shard_map/s,lsai->lai/dot_general | solution.py:23
  72.2 0.1 copy.19
  72.3 0.9 copy.20
  73.2 0.5 broadcast
  73.8 4.4 %reduce = bf16[384,768]{1,0:T(8,128)(2,1)S(1)} reduce(bf16[384,1,768]{2,1,0:T(2,128)(2,1)S(1)} %bitcast.54, bf16[]{:T(256)} %broadcast), dimensions={1}, to_apply=%bitcast.51.reduce_sub_computation | reduce | bytes 1179650
  78.1 1.0 reshape.33
  79.1 5.6 %all-to-all-start.1 = ((bf16[16,2,9216]{2,1,0:T(2,128)(2,1)}), bf16[16,2,9216]{2,1,0:T(2,128)(2,1)S(1)}, u32[]{:S(2)}, u32[]{:S(2)}) async-start(bf16[16,2,9216]{2,1,0:T(2,128)(2,1)} %reshape.33), calls=%async_computation.1 | async-start | bytes 1179648 | tf_op jit(solution)/shard_map/all_to_all | solution.py:24
  84.7 0.0 reduce-scatter.2.cloned.1.call-start
  85.4 14.7 %all-to-all-done.1 = bf16[16,2,9216]{2,1,0:T(2,128)(2,1)S(1)} async-done(((bf16[16,2,9216]{2,1,0:T(2,128)(2,1)}), bf16[16,2,9216]{2,1,0:T(2,128)(2,1)S(1)}, u32[]{:S(2)}, u32[]{:S(2)}) %all-to-all-start.1) | async-done | bytes 589856 | tf_op jit(solution)/shard_map/all_to_all | solution.py:24
  100.1 0.5 reshape.34
  100.6 0.1 copy.14
  100.7 1.2 fusion.4
  101.8 0.0 reduce-scatter.2.cloned.1.call-update
  101.9 20.9 %reduce-scatter.2.cloned.1.call-done = f32[8,24,768]{2,1,0:T(8,128)} async-done(((f32[16,24,768]{2,1,0:T(8,128)}), f32[8,24,768]{2,1,0:T(8,128)}) %reduce-scatter.2.cloned.1.call-update) | async-done | bytes 589840 | tf_op jit(solution)/shard_map/reduce_scatter | solution.py:26
Async XLA Ops:
  6.5 64.3 %copy-start = (f32[3]{0:T(128)S(1)}, f32[3]{0:T(128)}, u32[]{:S(2)}) copy-start(f32[3]{0:T(128)} %param.9) | copy-start | bytes 40
  6.5 1.1 copy-start.1
  6.5 1.5 %copy-start.2 = (f32[16,24,768]{2,1,0:T(8,128)S(1)}, f32[16,24,768]{2,1,0:T(8,128)}, u32[]{:S(2)}) copy-start(f32[16,24,768]{2,1,0:T(8,128)} %param.7) | copy-start | bytes 3538948
  6.5 54.4 %all-gather.2.cloned.1.call-start = ((), (), s32[]{:S(2)}) async-start(), calls=%async_computation.3 | async-start | bytes 5308416 | tf_op jit(solution)/shard_map/all_gather | solution.py:14
  8.0 8.4 %copy-start.3 = (bf16[3,24,384]{2,1,0:T(8,128)(2,1)S(1)}, bf16[3,24,384]{2,1,0:T(8,128)(2,1)}, u32[]{:S(2)}) copy-start(bf16[3,24,384]{2,1,0:T(8,128)(2,1)} %param.11) | copy-start | bytes 165892
  8.9 36.5 %all-to-all-start = ((bf16[16,24,768]{2,1,0:T(8,128)(2,1)}), bf16[16,24,768]{2,1,0:T(8,128)(2,1)S(1)}, u32[]{:S(2)}, u32[]{:S(2)}) async-start(bf16[16,24,768]{2,1,0:T(8,128)(2,1)} %fusion.5), calls=%async_computation | async-start | bytes 1179648 | tf_op jit(solution)/shard_map/all_to_all | solution.py:10
  79.1 21.0 %all-to-all-start.1 = ((bf16[16,2,9216]{2,1,0:T(2,128)(2,1)}), bf16[16,2,9216]{2,1,0:T(2,128)(2,1)S(1)}, u32[]{:S(2)}, u32[]{:S(2)}) async-start(bf16[16,2,9216]{2,1,0:T(2,128)(2,1)} %reshape.33), calls=%async_computation.1 | async-start | bytes 1179648 | tf_op jit(solution)/shard_map/all_to_all | solution.py:24
  84.7 38.0 %reduce-scatter.2.cloned.1.call-start = ((), (), s32[]{:S(2)}) async-start(), calls=%async_computation.4 | async-start | bytes 1769472 | tf_op jit(solution)/shard_map/reduce_scatter | solution.py:26
Sparse Core Ops, SparseCore 0:
  8.9 52.0 all-gather.1
  102.0 20.7 reduce-scatter.1
where the time goes:
time: 130 us
  waiting for transfers between devices  51.8 us (40%)
  blocking collectives  29.1 us (22%)
  between operations  14.1 us (11%)
  starting transfers between devices  13.1 us (10%)
  local copies, waits for them, and re-layouts  7.76 us (6%)
  matrix products  7.27 us (6%)
  other arithmetic  6.47 us (5%)
    all_gather x1, blocking collectives, on_device(): lax.all_gather(lat_filter, 'col', axis=1, tiled=True)  29.1 us
    reduce_scatter x1, waiting for transfers between devices, on_device(): return lax.psum_scatter(terms, 'mem', scatter_dimension=0, tiled=True)  20.9 us
    all_gather x1, waiting for transfers between devices, on_device(): lax.all_gather(lon_filter, 'mem', axis=1, tiled=True)  15.5 us
    all_to_all x1, waiting for transfers between devices, on_device(): lax.all_to_all(filtered, 'col', split_axis=1, concat_axis=0, tiled=True)  14.7 us
    all_to_all x1, starting transfers between devices, on_device(): lax.all_to_all(schur, 'col', split_axis=0, concat_axis=1, tiled=True)  7.41 us
    dot_general x1, matrix products, on_device(): jnp.einsum('sab,lsbi->lsai', lax.all_gather(lat_filter, 'col', axis=1, ti...  5.91 us
    all_to_all x1, starting transfers between devices, on_device(): lax.all_to_all(filtered, 'col', split_axis=1, concat_axis=0, tiled=True)  5.62 us
    unnamed x1, other arithmetic  4.37 us
  transfers between devices with their start and end apart: 4, of which 3 were waited for; matrix products, arithmetic and copies ran while one was open for 1% of the time, Pallas kernels for 0%

commit v1 on v0

--- a/solution.py
+++ b/solution.py
@@ -1,7 +1,14 @@
+import functools
+
 import jax
 import jax.numpy as jnp
 from jax import lax
+from jax.experimental import pallas as pl
+from jax.experimental.pallas import tpu as pltpu
 from jax.sharding import PartitionSpec as P
+
+MESH = pl.DeviceIdType.MESH
+CORES = 2
 
 
 def on_device(perturbations, gradient, member_weights, scale_weights, lon_filter, lat_filter):
@@ -26,7 +33,317 @@
     return lax.psum_scatter(terms, "mem", scatter_dimension=0, tiled=True)
 
 
+def fused(
+    mems, cols, depth_z, pert_h, grad_h, mw, sw, lon_h, lat_h, out_h,
+    pert, grad, lon, lonr, schur, xr, xs, latr, latf, latb, zs, ff, fb, back, acc, tsend, trecv,
+    loads, lat_send, lat_recv, x_send, x_recv, lonx_send, lonx_recv, lons_send, lons_recv,
+    b_send, b_recv, t_send, t_recv, stores,
+):
+    levels, rows, _ = grad.shape
+    scales = lon.shape[0]
+    half = pert.shape[3]
+    group = levels // mems
+    m, me = lax.axis_index("mem"), lax.axis_index("col")
+    other = 1 - m
+    depth_y = cols // CORES // depth_z
+    q = lax.rem(me, CORES)
+    yi = lax.rem(me // CORES, depth_y)
+    zi = me // (CORES * depth_y)
+    sibling = me + 1 - 2 * q
+
+    def place(z, y, core):
+        return (z * depth_y + y) * CORES + core
+
+    def remote(src, dst, ssem, rsem, device):
+        return pltpu.make_async_remote_copy(
+            src_ref=src, dst_ref=dst, send_sem=ssem, recv_sem=rsem,
+            device_id=device, device_id_type=MESH,
+        )
+
+    lat_load = pltpu.make_async_copy(lat_h, latr.at[me], loads.at[0])
+    lat_load.start()
+    pert_loads = [
+        pltpu.make_async_copy(pert_h.at[0, :, :, pl.ds(h * half, half)], pert.at[h], loads.at[1 + h])
+        for h in range(2)
+    ]
+    grad_load = pltpu.make_async_copy(grad_h, grad, loads.at[3])
+    lon_load = pltpu.make_async_copy(lon_h, lon, loads.at[4])
+    for load in pert_loads:
+        load.start()
+    grad_load.start()
+    lon_load.start()
+
+    barrier = pltpu.get_barrier_semaphore()
+
+    def greet(d, carry):
+        peer = lax.rem(me + d, cols)
+        pl.semaphore_signal(barrier, inc=1, device_id=(m, peer), device_id_type=MESH)
+        return carry
+
+    lax.fori_loop(1, cols, greet, 0)
+    pl.semaphore_signal(barrier, inc=1, device_id=(other, me), device_id_type=MESH)
+
+    for load in pert_loads:
+        load.wait()
+    grad_load.wait()
+
+    def product(c, carry):
+        lev = lax.rem(c, mems) * group + c // mems
+        for h in range(2):
+            at = pl.ds(h * half, half)
+            schur[c, :, at] = (
+                pert[h, lev].astype(jnp.float32) * grad[lev, :, at]
+            ).astype(jnp.bfloat16)
+        return carry
+
+    lax.fori_loop(0, cols, product, 0)
+    lat_load.wait()
+    pl.semaphore_wait(barrier, cols)
+
+    lat_copies = []
+
+    def lat_push(c, peer):
+        copy = remote(
+            latr.at[c], latr.at[c], lat_send.at[len(lat_copies)], lat_recv.at[c], (m, peer)
+        )
+        copy.start()
+        lat_copies.append(copy)
+
+    def lat_arrived(c):
+        remote(latr.at[c], latr.at[c], lat_send.at[0], lat_recv.at[c], (m, sibling)).wait_recv()
+
+    for dz in range(1, depth_z):
+        lat_push(me, place(lax.rem(zi + dz, depth_z), yi, q))
+    for dy in range(1, depth_y):
+        lat_push(me, place(zi, lax.rem(yi + dy, depth_y), q))
+    lat_push(me, sibling)
+
+    def lon_push(s):
+        return remote(
+            lon_h.at[s, q], lonr.at[s, q], lonx_send.at[s], lonx_recv.at[s], (other, me)
+        )
+
+    for s in range(scales):
+        lon_push(s).start()
+
+    def x_push(k):
+        peer = lax.rem(me + 1 + lax.rem(k + cols // 2 - 1, cols - 1), cols)
+        return peer, remote(
+            schur.at[peer], xr.at[me], x_send.at[peer], x_recv.at[me], (m, peer)
+        )
+
+    def x_start(k, carry):
+        x_push(k)[1].start()
+        return carry
+
+    lax.fori_loop(0, cols - 1, x_start, 0)
+
+    for dz in range(1, depth_z):
+        c = place(lax.rem(zi + dz, depth_z), yi, q)
+        lat_arrived(c)
+        for dy in range(1, depth_y):
+            lat_push(c, place(zi, lax.rem(yi + dy, depth_y), q))
+        lat_push(c, sibling)
+    for dz in range(depth_z):
+        for dy in range(1, depth_y):
+            c = place(lax.rem(zi + dz, depth_z), lax.rem(yi + dy, depth_y), q)
+            lat_arrived(c)
+            lat_push(c, sibling)
+    for k in range(cols // CORES):
+        lat_arrived(k * CORES + 1 - q)
+    for c in range(cols):
+        for s in range(scales):
+            latf[s, c * rows:(c + 1) * rows, :] = latr[c, s].astype(jnp.float32)
+    for s in range(scales):
+        latb[s] = latf[s].astype(jnp.bfloat16)
+
+    def lon_pass(s):
+        return remote(
+            lonr.at[s, q], lonr.at[s, q], lons_send.at[s], lons_recv.at[s], (m, sibling)
+        )
+
+    def lon_forward(s):
+        lon_push(s).wait_recv()
+        lon_pass(s).start()
+
+    lon_forward(0)
+
+    xr[me] = schur[me]
+
+    def x_wait(k, carry):
+        peer = lax.rem(me + 1 + k, cols)
+        remote(schur.at[peer], xr.at[peer], x_send.at[peer], x_recv.at[peer], (m, peer)).wait_recv()
+        return carry
+
+    lax.fori_loop(0, cols - 1, x_wait, 0)
+    for c in range(cols):
+        ff[c * rows:(c + 1) * rows, :] = xr[c].astype(jnp.float32)
+    xs[...] = ff[...].astype(jnp.bfloat16)
+    for s in range(scales):
+        zs[s] = (
+            jnp.dot(latb[s], xs[...], preferred_element_type=jnp.float32) * sw[s]
+        ).astype(jnp.bfloat16)
+
+    def b_push(ih, k):
+        peer = lax.rem(me + 1 + lax.rem(k + cols // 2 - 1, cols - 1), cols)
+        return remote(
+            fb.at[ih, peer], back.at[ih, me], b_send.at[ih, peer], b_recv.at[ih, me], (m, peer)
+        )
+
+    def filter_half(ih, source):
+        total = None
+        for s in range(scales):
+            part = lax.dot_general(
+                zs[s], source[s].reshape(half, 2 * half), (((1,), (1,)), ((), ())),
+                preferred_element_type=jnp.float32,
+            )
+            total = part if total is None else total + part
+        for c in range(cols):
+            fb[ih, c] = total[c * rows:(c + 1) * rows, :].astype(jnp.bfloat16)
+        back[ih, me] = fb[ih, me]
+
+        def b_start(k, carry):
+            b_push(ih, k).start()
+            return carry
+
+        lax.fori_loop(0, cols - 1, b_start, 0)
+
+    lon_load.wait()
+    filter_half(m, lon)
+    for s in range(1, scales):
+        lon_forward(s)
+    for s in range(scales):
+        remote(
+            lonr.at[s, 1 - q], lonr.at[s, 1 - q], lons_send.at[s], lons_recv.at[s], (m, sibling)
+        ).wait_recv()
+    filter_half(other, lonr)
+
+    weight = mw[0]
+
+    def t_copy(ih, r):
+        return remote(
+            tsend.at[ih, r], trecv.at[ih, r], t_send.at[ih, r], t_recv.at[ih, r], (other, me)
+        )
+
+    for step in range(2):
+        ih = m if step == 0 else other
+
+        def term(c, lev, ih=ih):
+            @pl.when(c != me)
+            def _():
+                remote(
+                    fb.at[ih, c], back.at[ih, c], b_send.at[ih, c], b_recv.at[ih, c], (m, c)
+                ).wait_recv()
+
+            return weight * pert[ih, lev].astype(jnp.float32) * back[ih, c].astype(jnp.float32)
+
+        def sent(r, carry, ih=ih, term=term):
+            tsend[ih, r] = term(r * mems + other, other * group + r).astype(jnp.bfloat16)
+            t_copy(ih, r).start()
+            return carry
+
+        def kept(r, carry, ih=ih, term=term):
+            acc[r, :, pl.ds(pl.multiple_of(ih * half, 128), half)] = term(
+                r * mems + m, m * group + r
+            )
+            return carry
+
+        lax.fori_loop(0, group, sent, 0)
+        lax.fori_loop(0, group, kept, 0)
+
+    def finish(r, carry):
+        for h in range(2):
+            t_copy(h, r).wait_recv()
+            at = pl.ds(h * half, half)
+            acc[r, :, at] = acc[r, :, at] + trecv[h, r].astype(jnp.float32)
+        pltpu.make_async_copy(acc.at[r], out_h.at[r], stores.at[r]).start()
+        return carry
+
+    lax.fori_loop(0, group, finish, 0)
+
+    for copy in lat_copies:
+        copy.wait_send()
+    for s in range(scales):
+        lon_push(s).wait_send()
+        lon_pass(s).wait_send()
+
+    def drain(k, carry):
+        x_push(k)[1].wait_send()
+        for ih in range(2):
+            b_push(ih, k).wait_send()
+        return carry
+
+    lax.fori_loop(0, cols - 1, drain, 0)
+
+    def drain_terms(r, carry):
+        for h in range(2):
+            t_copy(h, r).wait_send()
+        pltpu.make_async_copy(acc.at[r], out_h.at[r], stores.at[r]).wait()
+        return carry
+
+    lax.fori_loop(0, group, drain_terms, 0)
+
+
+def kernel_form(mems, cols, perturbations, gradient, member_weights, scale_weights, lon_filter, lat_filter):
+    levels, rows, nlon = gradient.shape
+    scales, lon_rows, _ = lon_filter.shape
+    nlat = lat_filter.shape[2]
+    half = nlon // 2
+    group = levels // mems
+    chips = cols // CORES
+    depth_z = 4 if chips % 4 == 0 else 1
+    depth_y = chips // depth_z
+    lat_sends = (depth_z - 1) + (depth_y - 1) + 1 + (depth_z - 1) * depth_y + depth_z * (depth_y - 1)
+    dma = pltpu.SemaphoreType.DMA
+    bf, f32 = jnp.bfloat16, jnp.float32
+    anywhere = pl.BlockSpec(memory_space=pl.ANY)
+    scalars = pl.BlockSpec(memory_space=pltpu.SMEM)
+    return pl.pallas_call(
+        functools.partial(fused, mems, cols, depth_z),
+        out_shape=jax.ShapeDtypeStruct((group, rows, nlon), f32),
+        in_specs=[anywhere, anywhere, scalars, scalars, anywhere, anywhere],
+        out_specs=anywhere,
+        scratch_shapes=[
+            pltpu.VMEM((2, levels, rows, half), bf),
+            pltpu.VMEM((levels, rows, nlon), f32),
+            pltpu.VMEM((scales, 2, lon_rows // 2, nlon), bf),
+            pltpu.VMEM((scales, 2, lon_rows // 2, nlon), bf),
+            pltpu.VMEM((cols, rows, nlon), bf),
+            pltpu.VMEM((cols, rows, nlon), bf),
+            pltpu.VMEM((nlat, nlon), bf),
+            pltpu.VMEM((cols, scales, rows, nlat), bf),
+            pltpu.VMEM((scales, nlat, nlat), f32),
+            pltpu.VMEM((scales, nlat, nlat), bf),
+            pltpu.VMEM((scales, nlat, nlon), bf),
+            pltpu.VMEM((nlat, nlon), f32),
+            pltpu.VMEM((2, cols, rows, half), bf),
+            pltpu.VMEM((2, cols, rows, half), bf),
+            pltpu.VMEM((group, rows, nlon), f32),
+            pltpu.VMEM((2, group, rows, half), bf),
+            pltpu.VMEM((2, group, rows, half), bf),
+            dma((5,)), dma((lat_sends,)), dma((cols,)), dma((cols,)), dma((cols,)),
+            dma((scales,)), dma((scales,)), dma((scales,)), dma((scales,)),
+            dma((2, cols)), dma((2, cols)), dma((2, group)), dma((2, group)), dma((group,)),
+        ],
+        compiler_params=pltpu.CompilerParams(
+            collective_id=0, has_side_effects=True, vmem_limit_bytes=48 * 1024 * 1024
+        ),
+    )(
+        perturbations, gradient, member_weights, scale_weights,
+        lon_filter.reshape(scales, 2, lon_rows // 2, nlon), lat_filter,
+    )
+
+
 def solution(mesh):
+    mems, cols = mesh.shape["mem"], mesh.shape["col"]
+
+    def step(perturbations, gradient, *rest):
+        levels, rows, nlon = gradient.shape
+        fits = mems == 2 and levels == cols and rows % 8 == 0 and nlon % 256 == 0
+        if not fits:
+            return on_device(perturbations, gradient, *rest)
+        return kernel_form(mems, cols, perturbations, gradient, *rest)
+
     placed = (
         P("mem", None, "col", None),
         P(None, "col", None),
@@ -36,5 +353,5 @@
         P(None, "col", None),
     )
     return jax.shard_map(
-        on_device, mesh=mesh, in_specs=placed, out_specs=P("mem", "col", None), check_vma=False
+        step, mesh=mesh, in_specs=placed, out_specs=P("mem", "col", None), check_vma=False
     )

time: 130 us -> 56.8 us (0.44)
  waiting for transfers between devices: 51.8 us -> 0 us
  Pallas kernels: 0 us -> 49.8 us
  blocking collectives: 29.1 us -> 0 us
  between operations: 14.1 us -> 0.67 us
  starting transfers between devices: 13.1 us -> 0 us
  matrix products: 7.27 us -> 0 us
  other arithmetic: 6.47 us -> 0 us
  local copies, waits for them, and re-layouts: 7.76 us -> 6.09 us
    pallas_call x0 -> x1, Pallas kernels: none -> 49.8 us  [kernel_form(): pl.pallas_call(functools.partial(fused, mems, cols, depth_z), out_shape=j...]
    all_gather x1 -> x0, blocking collectives: 29.1 us -> none  [on_device(): lax.all_gather(lat_filter, 'col', axis=1, tiled=True)]
    reduce_scatter x1 -> x0, waiting for transfers between devices: 20.9 us -> none  [on_device(): return lax.psum_scatter(terms, 'mem', scatter_dimension=0, tiled=True)]
    all_gather x1 -> x0, waiting for transfers between devices: 15.5 us -> none  [on_device(): lax.all_gather(lon_filter, 'mem', axis=1, tiled=True)]
    all_to_all x2 -> x0, waiting for transfers between devices: 14.7 us -> none  [the longest x1 14.7 us: on_device(): lax.all_to_all(filtered, 'col', split_axis=1, concat_axis=0, tiled=True)]
    all_to_all x2 -> x0, starting transfers between devices: 13 us -> none  [the longest x1 7.41 us: on_device(): lax.all_to_all(schur, 'col', split_axis=0, concat_axis=1, tiled=True)]
    dot_general x2 -> x0, matrix products: 7.27 us -> none  [the longest x1 5.91 us: on_device(): jnp.einsum('sab,lsbi->lsai', lax.all_gather(lat_filter, 'col', axis=1, ti...]
    unnamed x1 -> x0, other arithmetic: 4.37 us -> none
  transfers between devices with their start and end apart: 4 -> 0, of which waited for: 3 -> 0; matrix products, arithmetic and copies ran while one was open for 1% -> 0% of each run, Pallas kernels for 0% -> 0%
where the time goes in v1:
time: 56.8 us; the launch traced here: 56.6 us
  Pallas kernels  49.8 us (88%)
  local copies, waits for them, and re-layouts  6.09 us (11%)
  between operations  0.67 us (1%)
    pallas_call x1, Pallas kernels, kernel_form(): pl.pallas_call(functools.partial(fused, mems, cols, depth_z), out_shape=j...  49.8 us
    unnamed x11, local copies, waits for them, and re-layouts  6.09 us

profile of v1, /device:TPU:0, one launch (start us, length us, event | category | flops | bytes accessed | tf_op | source)
XLA Modules:
  0.0 56.6 jit_solution(14543745204812757631)
XLA Ops:
  0.7 0.0 copy-start
  0.7 1.5 %copy-done = bf16[3,384,768]{2,1,0:T(8,128)(2,1)S(1)} copy-done((bf16[3,384,768]{2,1,0:T(8,128)(2,1)S(1)}, bf16[3,384,768]{2,1,0:T(8,128)(2,1)}, u32[]{:S(2)}) %copy-start) | copy-done | bytes 1769496
  2.1 0.0 copy-start.1
  2.1 1.3 %copy-done.1 = f32[16,24,768]{2,1,0:T(8,128)S(1)} copy-done((f32[16,24,768]{2,1,0:T(8,128)S(1)}, f32[16,24,768]{2,1,0:T(8,128)}, u32[]{:S(2)}) %copy-start.1) | copy-done | bytes 1179672
  3.4 0.0 copy-start.2
  3.4 1.1 %copy-done.2 = bf16[1,16,24,768]{3,2,1,0:T(8,128)(2,1)S(1)} copy-done((bf16[1,16,24,768]{3,2,1,0:T(8,128)(2,1)S(1)}, bf16[1,16,24,768]{3,2,1,0:T(8,128)(2,1)}, u32[]{:S(2)}) %copy-start.2) | copy-done | bytes 589848
  4.5 0.0 copy-start.3
  4.5 0.8 %copy-done.3 = bf16[3,24,384]{2,1,0:T(8,128)(2,1)S(1)} copy-done((bf16[3,24,384]{2,1,0:T(8,128)(2,1)S(1)}, bf16[3,24,384]{2,1,0:T(8,128)(2,1)}, u32[]{:S(2)}) %copy-start.3) | copy-done | bytes 55320
  5.3 0.0 copy-start.4
  5.3 0.7 %copy-done.4 = f32[3]{0:T(128)S(1)} copy-done((f32[3]{0:T(128)S(1)}, f32[3]{0:T(128)}, u32[]{:S(2)}) %copy-start.4) | copy-done | bytes 36
  5.9 49.8 %shard_map.64 = f32[8,24,768]{2,1,0:T(8,128)S(1)} custom-call(bf16[1,16,24,768]{3,2,1,0:T(8,128)(2,1)S(1)} %copy-done.2, f32[16,24,768]{2,1,0:T(8,128)S(1)} %copy-done.1, f32[1]{0:T(128)S(6)} %copy.8.mw, f32[3]{0:T(128)S(1)} %copy-done.4, bf16[3,2,192,768]{3,2,1,0:T(8,128)(2,1)S(1)} %bitcast.1, bf16[3,24,384]{2,1,0:T(8,128)(2,1)S(1)} %copy-done.3), custom_call_target="tpu_custom_call" | custom-call | tf_op jit(solution)/shard_map/pallas_call | solution.py:301
  55.7 0.8 %copy.9 = f32[8,24,768]{2,1,0:T(8,128)} copy(f32[8,24,768]{2,1,0:T(8,128)S(1)} %shard_map.64) | data formatting | bytes 1179648
Async XLA Ops:
  0.7 1.5 %copy-start = (bf16[3,384,768]{2,1,0:T(8,128)(2,1)S(1)}, bf16[3,384,768]{2,1,0:T(8,128)(2,1)}, u32[]{:S(2)}) copy-start(bf16[3,384,768]{2,1,0:T(8,128)(2,1)} %param.10) | copy-start | bytes 5308420
  2.1 1.3 %copy-start.1 = (f32[16,24,768]{2,1,0:T(8,128)S(1)}, f32[16,24,768]{2,1,0:T(8,128)}, u32[]{:S(2)}) copy-start(f32[16,24,768]{2,1,0:T(8,128)} %grad_h.1) | copy-start | bytes 3538948
  3.4 1.1 %copy-start.2 = (bf16[1,16,24,768]{3,2,1,0:T(8,128)(2,1)S(1)}, bf16[1,16,24,768]{3,2,1,0:T(8,128)(2,1)}, u32[]{:S(2)}) copy-start(bf16[1,16,24,768]{3,2,1,0:T(8,128)(2,1)} %pert_h.1) | copy-start | bytes 1769476
  4.5 0.8 %copy-start.3 = (bf16[3,24,384]{2,1,0:T(8,128)(2,1)S(1)}, bf16[3,24,384]{2,1,0:T(8,128)(2,1)}, u32[]{:S(2)}) copy-start(bf16[3,24,384]{2,1,0:T(8,128)(2,1)} %lat_h.1) | copy-start | bytes 165892
  5.3 0.7 %copy-start.4 = (f32[3]{0:T(128)S(1)}, f32[3]{0:T(128)}, u32[]{:S(2)}) copy-start(f32[3]{0:T(128)} %sw.1) | copy-start | bytes 40

commit v2 on v1

--- a/solution.py
+++ b/solution.py
@@ -34,10 +34,10 @@
 
 
 def fused(
-    mems, cols, depth_z, pert_h, grad_h, mw, sw, lon_h, lat_h, out_h,
-    pert, grad, lon, lonr, schur, xr, xs, latr, latf, latb, zs, ff, fb, back, acc, tsend, trecv,
+    mems, cols, depth_z, pert_h, grad_h, mw, sw, lon_h, lat_h, acc, trecv,
+    pert, grad, lon, lonr, schur, xr, xs, latr, latf, latb, zs, ff, fb, back, tsend,
     loads, lat_send, lat_recv, x_send, x_recv, lonx_send, lonx_recv, lons_send, lons_recv,
-    b_send, b_recv, t_send, t_recv, stores,
+    b_send, b_recv, t_send, t_recv,
 ):
     levels, rows, _ = grad.shape
     scales = lon.shape[0]
@@ -91,7 +91,7 @@
         lev = lax.rem(c, mems) * group + c // mems
         for h in range(2):
             at = pl.ds(h * half, half)
-            schur[c, :, at] = (
+            schur[h, c] = (
                 pert[h, lev].astype(jnp.float32) * grad[lev, :, at]
             ).astype(jnp.bfloat16)
         return carry
@@ -102,53 +102,62 @@
 
     lat_copies = []
 
-    def lat_push(c, peer):
+    carrier = q == m
+
+    def lat_push(c, device, when=None):
         copy = remote(
-            latr.at[c], latr.at[c], lat_send.at[len(lat_copies)], lat_recv.at[c], (m, peer)
-        )
-        copy.start()
-        lat_copies.append(copy)
+            latr.at[c], latr.at[c], lat_send.at[len(lat_copies)], lat_recv.at[c], device
+        )
+        lat_copies.append((copy, when))
+        if when is None:
+            copy.start()
+        else:
+            pl.when(when)(copy.start)
 
     def lat_arrived(c):
         remote(latr.at[c], latr.at[c], lat_send.at[0], lat_recv.at[c], (m, sibling)).wait_recv()
 
     for dz in range(1, depth_z):
-        lat_push(me, place(lax.rem(zi + dz, depth_z), yi, q))
+        lat_push(me, (m, place(lax.rem(zi + dz, depth_z), yi, q)), carrier)
     for dy in range(1, depth_y):
-        lat_push(me, place(zi, lax.rem(yi + dy, depth_y), q))
-    lat_push(me, sibling)
+        lat_push(me, (m, place(zi, lax.rem(yi + dy, depth_y), q)))
+    lat_push(me, (m, sibling))
 
     def lon_push(s):
         return remote(
             lon_h.at[s, q], lonr.at[s, q], lonx_send.at[s], lonx_recv.at[s], (other, me)
         )
 
-    for s in range(scales):
-        lon_push(s).start()
-
-    def x_push(k):
+    lon_push(0).start()
+
+    def x_push(h, k):
         peer = lax.rem(me + 1 + lax.rem(k + cols // 2 - 1, cols - 1), cols)
-        return peer, remote(
-            schur.at[peer], xr.at[me], x_send.at[peer], x_recv.at[me], (m, peer)
-        )
-
-    def x_start(k, carry):
-        x_push(k)[1].start()
-        return carry
-
-    lax.fori_loop(0, cols - 1, x_start, 0)
+        return remote(
+            schur.at[h, peer], xr.at[h, me], x_send.at[h, peer], x_recv.at[h, me], (m, peer)
+        )
+
+    for h in range(2):
+
+        def x_start(k, carry, h=h):
+            x_push(h, k).start()
+            return carry
+
+        lax.fori_loop(0, cols - 1, x_start, 0)
 
     for dz in range(1, depth_z):
         c = place(lax.rem(zi + dz, depth_z), yi, q)
         lat_arrived(c)
+        lat_push(c, (other, me), carrier)
         for dy in range(1, depth_y):
-            lat_push(c, place(zi, lax.rem(yi + dy, depth_y), q))
-        lat_push(c, sibling)
+            lat_push(c, (m, place(zi, lax.rem(yi + dy, depth_y), q)))
+        lat_push(c, (m, sibling))
+    for s in range(1, scales):
+        lon_push(s).start()
     for dz in range(depth_z):
         for dy in range(1, depth_y):
             c = place(lax.rem(zi + dz, depth_z), lax.rem(yi + dy, depth_y), q)
             lat_arrived(c)
-            lat_push(c, sibling)
+            lat_push(c, (m, sibling))
     for k in range(cols // CORES):
         lat_arrived(k * CORES + 1 - q)
     for c in range(cols):
@@ -168,21 +177,25 @@
 
     lon_forward(0)
 
-    xr[me] = schur[me]
-
-    def x_wait(k, carry):
-        peer = lax.rem(me + 1 + k, cols)
-        remote(schur.at[peer], xr.at[peer], x_send.at[peer], x_recv.at[peer], (m, peer)).wait_recv()
-        return carry
-
-    lax.fori_loop(0, cols - 1, x_wait, 0)
-    for c in range(cols):
-        ff[c * rows:(c + 1) * rows, :] = xr[c].astype(jnp.float32)
-    xs[...] = ff[...].astype(jnp.bfloat16)
-    for s in range(scales):
-        zs[s] = (
-            jnp.dot(latb[s], xs[...], preferred_element_type=jnp.float32) * sw[s]
-        ).astype(jnp.bfloat16)
+    for h in range(2):
+        xr[h, me] = schur[h, me]
+
+        def x_wait(k, carry, h=h):
+            peer = lax.rem(me + 1 + k, cols)
+            remote(
+                schur.at[h, peer], xr.at[h, peer], x_send.at[h, peer], x_recv.at[h, peer], (m, peer)
+            ).wait_recv()
+            return carry
+
+        lax.fori_loop(0, cols - 1, x_wait, 0)
+        at = pl.ds(h * half, half)
+        for c in range(cols):
+            ff[c * rows:(c + 1) * rows, at] = xr[h, c].astype(jnp.float32)
+        xs[:, at] = ff[:, at].astype(jnp.bfloat16)
+        for s in range(scales):
+            zs[s, :, at] = (
+                jnp.dot(latb[s], xs[:, at], preferred_element_type=jnp.float32) * sw[s]
+            ).astype(jnp.bfloat16)
 
     def b_push(ih, k):
         peer = lax.rem(me + 1 + lax.rem(k + cols // 2 - 1, cols - 1), cols)
@@ -222,54 +235,70 @@
 
     def t_copy(ih, r):
         return remote(
-            tsend.at[ih, r], trecv.at[ih, r], t_send.at[ih, r], t_recv.at[ih, r], (other, me)
-        )
-
-    for step in range(2):
-        ih = m if step == 0 else other
-
-        def term(c, lev, ih=ih):
-            @pl.when(c != me)
-            def _():
-                remote(
-                    fb.at[ih, c], back.at[ih, c], b_send.at[ih, c], b_recv.at[ih, c], (m, c)
-                ).wait_recv()
-
-            return weight * pert[ih, lev].astype(jnp.float32) * back[ih, c].astype(jnp.float32)
-
-        def sent(r, carry, ih=ih, term=term):
-            tsend[ih, r] = term(r * mems + other, other * group + r).astype(jnp.bfloat16)
+            tsend.at[ih, r], trecv.at[r, :, pl.ds(pl.multiple_of(ih * half, 128), half)],
+            t_send.at[ih, r], t_recv.at[ih, r], (other, me)
+        )
+
+    chips = cols // CORES
+
+    def source_of(k, core):
+        p, y = k // depth_y, lax.rem(yi + lax.rem(k, depth_y), depth_y)
+        if depth_z == 4:
+            low = lax.rem(p, 2)
+            z = lax.rem(zi + low * (1 - 2 * lax.rem(zi, 2)) + 2 * (p // 2), depth_z)
+        else:
+            z = lax.rem(zi + p, depth_z)
+        return place(z, y, core)
+
+    def term(ih, c, lev):
+        @pl.when(c != me)
+        def _():
+            remote(
+                fb.at[ih, c], back.at[ih, c], b_send.at[ih, c], b_recv.at[ih, c], (m, c)
+            ).wait_recv()
+
+        return weight * pert[ih, lev].astype(jnp.float32) * back[ih, c].astype(jnp.float32)
+
+    for ih in (m, other):
+
+        def sent(k, carry, ih=ih):
+            c = source_of(k, other)
+            r = c // mems
+            tsend[ih, r] = term(ih, c, other * group + r).astype(jnp.bfloat16)
             t_copy(ih, r).start()
             return carry
 
-        def kept(r, carry, ih=ih, term=term):
-            acc[r, :, pl.ds(pl.multiple_of(ih * half, 128), half)] = term(
-                r * mems + m, m * group + r
-            )
-            return carry
-
-        lax.fori_loop(0, group, sent, 0)
-        lax.fori_loop(0, group, kept, 0)
+        lax.fori_loop(0, chips, sent, 0)
+
+    for ih in (m, other):
+
+        def kept(k, carry, ih=ih):
+            c = source_of(k, m)
+            r = c // mems
+            acc[r, :, pl.ds(pl.multiple_of(ih * half, 128), half)] = term(ih, c, m * group + r)
+            return carry
+
+        lax.fori_loop(0, chips, kept, 0)
 
     def finish(r, carry):
         for h in range(2):
             t_copy(h, r).wait_recv()
-            at = pl.ds(h * half, half)
-            acc[r, :, at] = acc[r, :, at] + trecv[h, r].astype(jnp.float32)
-        pltpu.make_async_copy(acc.at[r], out_h.at[r], stores.at[r]).start()
         return carry
 
     lax.fori_loop(0, group, finish, 0)
 
-    for copy in lat_copies:
-        copy.wait_send()
+    for copy, when in lat_copies:
+        if when is None:
+            copy.wait_send()
+        else:
+            pl.when(when)(copy.wait_send)
     for s in range(scales):
         lon_push(s).wait_send()
         lon_pass(s).wait_send()
 
     def drain(k, carry):
-        x_push(k)[1].wait_send()
         for ih in range(2):
+            x_push(ih, k).wait_send()
             b_push(ih, k).wait_send()
         return carry
 
@@ -278,7 +307,6 @@
     def drain_terms(r, carry):
         for h in range(2):
             t_copy(h, r).wait_send()
-        pltpu.make_async_copy(acc.at[r], out_h.at[r], stores.at[r]).wait()
         return carry
 
     lax.fori_loop(0, group, drain_terms, 0)
@@ -293,23 +321,26 @@
     chips = cols // CORES
     depth_z = 4 if chips % 4 == 0 else 1
     depth_y = chips // depth_z
-    lat_sends = (depth_z - 1) + (depth_y - 1) + 1 + (depth_z - 1) * depth_y + depth_z * (depth_y - 1)
+    lat_sends = depth_z + depth_y - 1 + (depth_z - 1) * (depth_y + 1) + depth_z * (depth_y - 1)
     dma = pltpu.SemaphoreType.DMA
     bf, f32 = jnp.bfloat16, jnp.float32
-    anywhere = pl.BlockSpec(memory_space=pl.ANY)
+    anywhere = pl.BlockSpec(memory_space=pltpu.MemorySpace.HBM)
     scalars = pl.BlockSpec(memory_space=pltpu.SMEM)
-    return pl.pallas_call(
+    own, received = pl.pallas_call(
         functools.partial(fused, mems, cols, depth_z),
-        out_shape=jax.ShapeDtypeStruct((group, rows, nlon), f32),
+        out_shape=[
+            jax.ShapeDtypeStruct((group, rows, nlon), f32),
+            jax.ShapeDtypeStruct((group, rows, nlon), bf),
+        ],
         in_specs=[anywhere, anywhere, scalars, scalars, anywhere, anywhere],
-        out_specs=anywhere,
+        out_specs=[pl.BlockSpec(memory_space=pltpu.VMEM)] * 2,
         scratch_shapes=[
             pltpu.VMEM((2, levels, rows, half), bf),
             pltpu.VMEM((levels, rows, nlon), f32),
             pltpu.VMEM((scales, 2, lon_rows // 2, nlon), bf),
             pltpu.VMEM((scales, 2, lon_rows // 2, nlon), bf),
-            pltpu.VMEM((cols, rows, nlon), bf),
-            pltpu.VMEM((cols, rows, nlon), bf),
+            pltpu.VMEM((2, cols, rows, half), bf),
+            pltpu.VMEM((2, cols, rows, half), bf),
             pltpu.VMEM((nlat, nlon), bf),
             pltpu.VMEM((cols, scales, rows, nlat), bf),
             pltpu.VMEM((scales, nlat, nlat), f32),
@@ -318,20 +349,19 @@
             pltpu.VMEM((nlat, nlon), f32),
             pltpu.VMEM((2, cols, rows, half), bf),
             pltpu.VMEM((2, cols, rows, half), bf),
-            pltpu.VMEM((group, rows, nlon), f32),
             pltpu.VMEM((2, group, rows, half), bf),
-            pltpu.VMEM((2, group, rows, half), bf),
-            dma((5,)), dma((lat_sends,)), dma((cols,)), dma((cols,)), dma((cols,)),
+            dma((5,)), dma((lat_sends,)), dma((cols,)), dma((2, cols)), dma((2, cols)),
             dma((scales,)), dma((scales,)), dma((scales,)), dma((scales,)),
-            dma((2, cols)), dma((2, cols)), dma((2, group)), dma((2, group)), dma((group,)),
+            dma((2, cols)), dma((2, cols)), dma((2, group)), dma((2, group)),
         ],
         compiler_params=pltpu.CompilerParams(
-            collective_id=0, has_side_effects=True, vmem_limit_bytes=48 * 1024 * 1024
+            collective_id=0, has_side_effects=True, vmem_limit_bytes=60 * 1024 * 1024
         ),
     )(
         perturbations, gradient, member_weights, scale_weights,
         lon_filter.reshape(scales, 2, lon_rows // 2, nlon), lat_filter,
     )
+    return own + received.astype(f32)
 
 
 def solution(mesh):

time: 56.8 us -> 50 us (0.88)
  local copies, waits for them, and re-layouts: 6.09 us -> 0 us
  Pallas kernels: 49.8 us -> 47.1 us
  other arithmetic: 0 us -> 2.01 us
    unnamed x11 -> x0, local copies, waits for them, and re-layouts: 6.09 us -> none
    pallas_call x1, Pallas kernels: 49.8 us -> 47.1 us  [kernel_form(): pl.pallas_call(functools.partial(fused, mems, cols, depth_z), out_shape=[...]
    add x0 -> x1, other arithmetic: none -> 2.01 us  [kernel_form(): return own + received.astype(f32)]
where the time goes in v2:
time: 50 us; the launch traced here: 49.8 us
  Pallas kernels  47.1 us (94%)
  other arithmetic  2.01 us (4%)
  between operations  0.66 us (1%)
    pallas_call x1, Pallas kernels, kernel_form(): pl.pallas_call(functools.partial(fused, mems, cols, depth_z), out_shape=[...  47.1 us
    add x1, other arithmetic, kernel_form(): return own + received.astype(f32)  2.01 us

profile of v2, /device:TPU:0, one launch (start us, length us, event | category | flops | bytes accessed | tf_op | source)
XLA Modules:
  0.0 49.8 jit_solution(15807321605606118097)
XLA Ops:
  0.7 47.1 %shard_map.64 = (f32[8,24,768]{2,1,0:T(8,128)}, bf16[8,24,768]{2,1,0:T(8,128)(2,1)}) custom-call(bf16[1,16,24,768]{3,2,1,0:T(8,128)(2,1)} %pert_h.1, f32[16,24,768]{2,1,0:T(8,128)} %grad_h.1, f32[1]{0:T(128)S(6)} %copy.7.mw, f32[3]{0:T(128)} %sw.1, bf16[3,2,192,768]{3,2,1,0:T(8,128)(2,1)} %bitcast.1, bf16[3,24,384]{2,1,0:T(8,128)(2,1)} %lat_h.1), custom_call_target="tpu_custom_call" | custom-call | tf_op jit(solution)/shard_map/pallas_call | solution.py:329
  47.8 2.0 %convert_add_fusion = f32[8,24,768]{2,1,0:T(8,128)} fusion(f32[8,24,768]{2,1,0:T(8,128)} %get-tuple-element.7, bf16[8,24,768]{2,1,0:T(8,128)(2,1)} %get-tuple-element.8), kind=kLoop, calls=%fused_computation | loop fusion | flops 294912 | bytes 1474560 | tf_op jit(solution)/shard_map/add | solution.py:364

commit v3 on v2

--- a/solution.py
+++ b/solution.py
@@ -76,7 +76,7 @@
     barrier = pltpu.get_barrier_semaphore()
 
     def greet(d, carry):
-        peer = lax.rem(me + d, cols)
+        peer = lax.rem(me + 1 + lax.rem(d + cols // 2 - 2, cols - 1), cols)
         pl.semaphore_signal(barrier, inc=1, device_id=(m, peer), device_id_type=MESH)
         return carry
 
@@ -198,7 +198,7 @@
             ).astype(jnp.bfloat16)
 
     def b_push(ih, k):
-        peer = lax.rem(me + 1 + lax.rem(k + cols // 2 - 1, cols - 1), cols)
+        peer = lax.rem(me + 1 + lax.rem(cols + cols // 2 - 2 - k, cols - 1), cols)
         return remote(
             fb.at[ih, peer], back.at[ih, me], b_send.at[ih, peer], b_recv.at[ih, me], (m, peer)
         )

time: 50 us -> 48.9 us (0.978)
  Pallas kernels: 47.1 us -> 46.1 us
    pallas_call x1, Pallas kernels: 47.1 us -> 46.1 us  [kernel_form(): pl.pallas_call(functools.partial(fused, mems, cols, depth_z), out_shape=[...]
where the time goes in v3:
time: 48.9 us; the launch traced here: 48.8 us
  Pallas kernels  46.1 us (94%)
  other arithmetic  2.01 us (4%)
  between operations  0.66 us (1%)
    pallas_call x1, Pallas kernels, kernel_form(): pl.pallas_call(functools.partial(fused, mems, cols, depth_z), out_shape=[...  46.1 us
    add x1, other arithmetic, kernel_form(): return own + received.astype(f32)  2.01 us

profile of v3, /device:TPU:0, one launch (start us, length us, event | category | flops | bytes accessed | tf_op | source)
XLA Modules:
  0.0 48.8 jit_solution(9520491949336078857)
XLA Ops:
  0.7 46.1 %shard_map.64 = (f32[8,24,768]{2,1,0:T(8,128)}, bf16[8,24,768]{2,1,0:T(8,128)(2,1)}) custom-call(bf16[1,16,24,768]{3,2,1,0:T(8,128)(2,1)} %pert_h.1, f32[16,24,768]{2,1,0:T(8,128)} %grad_h.1, f32[1]{0:T(128)S(6)} %copy.7.mw, f32[3]{0:T(128)} %sw.1, bf16[3,2,192,768]{3,2,1,0:T(8,128)(2,1)} %bitcast.1, bf16[3,24,384]{2,1,0:T(8,128)(2,1)} %lat_h.1), custom_call_target="tpu_custom_call" | custom-call | tf_op jit(solution)/shard_map/pallas_call | solution.py:329
  46.7 2.0 %convert_add_fusion = f32[8,24,768]{2,1,0:T(8,128)} fusion(f32[8,24,768]{2,1,0:T(8,128)} %get-tuple-element.7, bf16[8,24,768]{2,1,0:T(8,128)(2,1)} %get-tuple-element.8), kind=kLoop, calls=%fused_computation | loop fusion | flops 294912 | bytes 1474560 | tf_op jit(solution)/shard_map/add | solution.py:364
